TPU v7x, 512 devices: a whole 4x4x16 slice. The times are simulated.
512 devices in a mesh: pipe: 16 (over y, z_lo), dp: 32 (over z_hi, x, core).
Axes of the slice: x: 4, y: 4, z: 16 (z_hi: 4, z_lo: 4; z = z_hi * 4 + z_lo), core: 2. Of those that a mesh axis runs over, the one named last changes fastest.
Arguments:
- grad_out: bfloat16 [16, 2, 2, 128, 3584], P('pipe', None, None, 'dp'), may hold values from -6 to 6
- hidden: bfloat16 [16, 2, 2, 128, 9216], P('pipe', None, None, None, 'dp'), may hold values from -5 to 5
- weights: bfloat16 [16, 9216, 3584], P('pipe', 'dp'), may hold values from -5 to 5
- counts: int32 [16, 2, 2, 32], P('pipe', None, None, 'dp'), may hold values from 1 to 4
Outputs:
- grad_hidden: bfloat16 [16, 2, 2, 128, 9216], P('pipe', None, None, None, 'dp')
- new_weights: bfloat16 [16, 9216, 3584], P('pipe', 'dp')
All inputs are finite; a program needn't handle non-finite values.
Results may differ from a plain program's by a relative error of at most 0.0034.
Values may be sent and summed in bfloat16 or wider, within the bound.
No kernel may reach another device: no remote copies, remote signals or barrier semaphores. Data moves between devices by JAX's collectives and lax.ppermute only.
A program may use at most 64 MiB of HBM per device.

v0:
```python
import jax
import jax.numpy as jnp
from jax import lax
from jax.sharding import PartitionSpec as P

step_rate = 2.0


def from_partner(block, axis, apart):
    count = lax.axis_size(axis)
    route = []
    for low in range(count):
        high = low | 1 << apart
        if high != low and high < count:
            route += [(low, high), (high, low)]
    return lax.ppermute(block, axis, route)


def shards(grad_out, hidden, weights, counts):
    row_total = grad_out.shape[3]
    full_width = grad_out.shape[4]
    micro = hidden.shape[2]
    group_rows = hidden.shape[3]
    share = hidden.shape[4]
    scale_factor = float(full_width) ** (-0.5)
    slot_index = lax.broadcasted_iota(jnp.int32, (1, 1, 1, row_total), 3)
    live_rows = slot_index < counts
    masked = jnp.where(live_rows[..., None], grad_out, jnp.zeros_like(grad_out))
    own_weight = weights[0]
    pipe_bits = lax.axis_size("pipe").bit_length() - 1
    outgoing = jnp.concatenate(
        [masked[0, 1].reshape(micro, -1), hidden[0, 1].reshape(micro, -1)], axis=1
    )
    incoming = outgoing
    for fetch_bit_index in range(pipe_bits):
        incoming = from_partner(incoming, "pipe", fetch_bit_index)
    split_at = row_total * full_width
    mirror_masked = incoming[:, :split_at].reshape(micro, row_total, full_width)
    mirror_hidden = incoming[:, split_at:].reshape(micro, group_rows, share)
    mirror_masked, mirror_hidden = (mirror_masked, mirror_hidden)
    both_masked = jnp.stack([masked[0, 0], mirror_masked], axis=0)
    both_hidden = jnp.stack([hidden[0, 0], mirror_hidden], axis=0)
    piece = lax.all_gather(both_masked, "dp", axis=2, tiled=True)
    rows_out = jnp.einsum("rmkd,hd->rmkh", piece, own_weight, preferred_element_type=jnp.float32)
    grad_acc = rows_out
    weight_acc = jnp.einsum(
        "rmkh,rmkd->rhd", both_hidden, piece, preferred_element_type=jnp.float32
    )
    grad_acc, weight_acc = (grad_acc, weight_acc)
    grad_rows = (grad_acc * scale_factor).astype(jnp.bfloat16)
    partial_value = (weight_acc * scale_factor).astype(jnp.bfloat16)
    gradient = partial_value[0].astype(jnp.float32) + partial_value[1].astype(jnp.float32)
    new_weight = (own_weight.astype(jnp.float32) - step_rate * gradient).astype(jnp.bfloat16)
    returned = grad_rows[1]
    for bit_index in range(pipe_bits):
        returned = from_partner(returned, "pipe", bit_index)
    grad_hidden = jnp.stack([grad_rows[0], returned], axis=0)[None]
    return (grad_hidden, new_weight[None])


def solution(mesh):
    return jax.shard_map(
        shards,
        mesh=mesh,
        in_specs=(
            P("pipe", None, None, "dp", None),
            P("pipe", None, None, None, "dp"),
            P("pipe", "dp", None),
            P("pipe", None, None, "dp"),
        ),
        out_specs=(P("pipe", None, None, None, "dp"), P("pipe", "dp", None)),
        check_vma=False,
    )
```

profile of v0, /device:TPU:4, one launch (start us, length us, event | category | flops | bytes accessed | tf_op | source)
XLA Modules:
  0.0 193.9 jit_solution(3951308479756435278)
XLA Ops:
  7.2 0.0 all-gather.2.cloned.1.call-start
  7.2 0.7 iota_compare_fusion
  7.9 1.1 broadcast_select_fusion
  9.0 0.1 slice_bitcast_fusion.2
  9.0 1.0 slice_bitcast_fusion.1
  10.1 0.2 copy.9
  10.2 0.3 reshape_squeeze.7
  10.5 0.2 pad_maximum_fusion
  10.7 3.8 %collective-permute-start = (bf16[2,51200]{1,0:T(2,128)(2,1)S(1)}, bf16[2,51200]{1,0:T(2,128)(2,1)S(1)}, u32[]{:S(2)}, u32[]{:S(2)}) collective-permute-start(bf16[2,51200]{1,0:T(2,128)(2,1)S(1)} %pad_maximum_fusion), channel_id=1, source_target_pairs={{0,32},{32,0},{64,96},{96,64},{128,160},{160,128},{192,224},{224,1... | collective-permute-start | bytes 614408 | tf_op jit(solution)/shard_map/ppermute | solution.py:16
  14.6 5.1 %collective-permute-done = bf16[2,51200]{1,0:T(2,128)(2,1)S(1)} collective-permute-done((bf16[2,51200]{1,0:T(2,128)(2,1)S(1)}, bf16[2,51200]{1,0:T(2,128)(2,1)S(1)}, u32[]{:S(2)}, u32[]{:S(2)}) %collective-permute-start) | collective-permute-done | bytes 204832 | tf_op jit(solution)/shard_map/ppermute | solution.py:16
  19.6 5.2 %collective-permute-start.1 = (bf16[2,51200]{1,0:T(2,128)(2,1)S(1)}, bf16[2,51200]{1,0:T(2,128)(2,1)S(1)}, u32[]{:S(2)}, u32[]{:S(2)}) collective-permute-start(bf16[2,51200]{1,0:T(2,128)(2,1)S(1)} %collective-permute-done), channel_id=1, source_target_pairs={{0,64},{64,0},{32,96},{96,32},{128,192},{192,128},{160,224},{224,1... | collective-permute-start | bytes 614408 | tf_op jit(solution)/shard_map/ppermute | solution.py:16
  24.8 8.8 %collective-permute-done.1 = bf16[2,51200]{1,0:T(2,128)(2,1)S(1)} collective-permute-done((bf16[2,51200]{1,0:T(2,128)(2,1)S(1)}, bf16[2,51200]{1,0:T(2,128)(2,1)S(1)}, u32[]{:S(2)}, u32[]{:S(2)}) %collective-permute-start.1) | collective-permute-done | bytes 204832 | tf_op jit(solution)/shard_map/ppermute | solution.py:16
  33.6 3.5 %collective-permute-start.2 = (bf16[2,51200]{1,0:T(2,128)(2,1)S(1)}, bf16[2,51200]{1,0:T(2,128)(2,1)S(1)}, u32[]{:S(2)}, u32[]{:S(2)}) collective-permute-start(bf16[2,51200]{1,0:T(2,128)(2,1)S(1)} %collective-permute-done.1), channel_id=1, source_target_pairs={{0,128},{128,0},{32,160},{160,32},{64,192},{192,64},{96,224},{224,... | collective-permute-start | bytes 614408 | tf_op jit(solution)/shard_map/ppermute | solution.py:16
  37.1 4.4 %collective-permute-done.2 = bf16[2,51200]{1,0:T(2,128)(2,1)S(1)} collective-permute-done((bf16[2,51200]{1,0:T(2,128)(2,1)S(1)}, bf16[2,51200]{1,0:T(2,128)(2,1)S(1)}, u32[]{:S(2)}, u32[]{:S(2)}) %collective-permute-start.2) | collective-permute-done | bytes 204832 | tf_op jit(solution)/shard_map/ppermute | solution.py:16
  41.4 5.1 %collective-permute-start.3 = (bf16[2,51200]{1,0:T(2,128)(2,1)S(1)}, bf16[2,51200]{1,0:T(2,128)(2,1)S(1)}, u32[]{:S(2)}, u32[]{:S(2)}) collective-permute-start(bf16[2,51200]{1,0:T(2,128)(2,1)S(1)} %collective-permute-done.2), channel_id=1, source_target_pairs={{0,256},{256,0},{32,288},{288,32},{64,320},{320,64},{96,352},{352,... | collective-permute-start | bytes 614408 | tf_op jit(solution)/shard_map/ppermute | solution.py:16
  46.5 4.0 %collective-permute-done.3 = bf16[2,51200]{1,0:T(2,128)(2,1)S(1)} collective-permute-done((bf16[2,51200]{1,0:T(2,128)(2,1)S(1)}, bf16[2,51200]{1,0:T(2,128)(2,1)S(1)}, u32[]{:S(2)}, u32[]{:S(2)}) %collective-permute-start.3) | collective-permute-done | bytes 204832 | tf_op jit(solution)/shard_map/ppermute | solution.py:16
  50.6 0.8 pad_maximum_fusion.1
  51.4 0.0 all-gather.2.cloned.1.call-update
  51.5 93.9 %all-gather.2.cloned.1.call-done = bf16[2,2,128,3584]{3,1,0,2:T(2,128)(2,1)} async-done(((bf16[2,2,4,3584]{3,1,0,2:T(2,128)(2,1)}), bf16[2,2,128,3584]{3,1,0,2:T(2,128)(2,1)}) %all-gather.2.cloned.1.call-update) | async-done | bytes 3670032 | tf_op jit(solution)/shard_map/all_gather | solution.py:43
  145.4 4.0 %fusion.10 = bf16[2,2,128,288]{2,3,1,0:T(8,128)(2,1)S(1)} fusion(bf16[1,288,3584]{2,1,0:T(8,128)(2,1)} %param.6, bf16[2,2,128,3584]{3,1,0,2:T(2,128)(2,1)} %all-gather.2.cloned.1.call-done), kind=kOutput, calls=%fused_computation.8 | convolution fusion | flops 1057259520 | bytes 6029312 | tf_op jit(solution)/shard_map/rmkd,hd->rmkh/dot_general | solution.py:44
  149.4 1.9 collective-permute-start.4
  151.3 6.0 %collective-permute-done.4 = bf16[2,128,288]{1,2,0:T(8,128)(2,1)S(1)} collective-permute-done((bf16[2,128,288]{1,2,0:T(8,128)(2,1)S(1)}, bf16[2,128,288]{1,2,0:T(8,128)(2,1)S(1)}, u32[]{:S(2)}, u32[]{:S(2)}) %collective-permute-start.4) | collective-permute-done | bytes 147488 | tf_op jit(solution)/shard_map/ppermute | solution.py:16
  157.3 3.5 %collective-permute-start.5 = (bf16[2,128,288]{1,2,0:T(8,128)(2,1)S(1)}, bf16[2,128,288]{1,2,0:T(8,128)(2,1)S(1)}, u32[]{:S(2)}, u32[]{:S(2)}) collective-permute-start(bf16[2,128,288]{1,2,0:T(8,128)(2,1)S(1)} %collective-permute-done.4), channel_id=1, source_target_pairs={{0,64},{64,0},{32,96},{96,32},{128,192},{192,128},{160,224},{224,1... | collective-permute-start | bytes 442376 | tf_op jit(solution)/shard_map/ppermute | solution.py:16
  160.8 0.1 slice.45
  160.9 0.3 stack_reshape.7
  161.2 0.2 copy.12
  161.4 7.1 %collective-permute-done.5 = bf16[2,128,288]{1,2,0:T(8,128)(2,1)S(1)} collective-permute-done((bf16[2,128,288]{1,2,0:T(8,128)(2,1)S(1)}, bf16[2,128,288]{1,2,0:T(8,128)(2,1)S(1)}, u32[]{:S(2)}, u32[]{:S(2)}) %collective-permute-start.5) | collective-permute-done | bytes 147488 | tf_op jit(solution)/shard_map/ppermute | solution.py:16
  168.5 4.9 %collective-permute-start.6 = (bf16[2,128,288]{1,2,0:T(8,128)(2,1)S(1)}, bf16[2,128,288]{1,2,0:T(8,128)(2,1)S(1)}, u32[]{:S(2)}, u32[]{:S(2)}) collective-permute-start(bf16[2,128,288]{1,2,0:T(8,128)(2,1)S(1)} %collective-permute-done.5), channel_id=1, source_target_pairs={{0,128},{128,0},{32,160},{160,32},{64,192},{192,64},{96,224},{224,... | collective-permute-start | bytes 442376 | tf_op jit(solution)/shard_map/ppermute | solution.py:16
  173.4 0.0 copy-start
  173.4 4.1 %fusion = bf16[2,288,3584]{2,1,0:T(8,128)(2,1)S(1)} fusion(bf16[2,2,128,3584]{3,1,0,2:T(2,128)(2,1)} %all-gather.2.cloned.1.call-done, bf16[1,2,128,288]{2,3,1,0:T(8,128)(2,1)S(1)} %copy.12, bf16[1,2,128,288]{2,3,1,0:T(8,128)(2,1)S(1)} %get-tuple-element.2), kind=kOutput, calls=%fused_computation.1 | convolution fusion | flops 1061240832 | bytes 8093696 | tf_op jit(solution)/shard_map/rmkh,rmkd->rhd/dot_general | solution.py:46
  177.5 0.0 collective-permute-done.6
  177.5 4.6 %collective-permute-start.7 = (bf16[2,128,288]{1,2,0:T(8,128)(2,1)S(1)}, bf16[2,128,288]{1,2,0:T(8,128)(2,1)S(1)}, u32[]{:S(2)}, u32[]{:S(2)}) collective-permute-start(bf16[2,128,288]{1,2,0:T(8,128)(2,1)S(1)} %collective-permute-done.6), channel_id=1, source_target_pairs={{0,256},{256,0},{32,288},{288,32},{64,320},{320,64},{96,352},{352,... | collective-permute-start | bytes 442376 | tf_op jit(solution)/shard_map/ppermute | solution.py:16
  182.1 0.0 copy-done
  182.1 2.2 %subtract_convert_fusion = bf16[1,288,3584]{2,1,0:T(8,128)(2,1)} fusion(bf16[1,288,3584]{2,1,0:T(8,128)(2,1)S(1)} %copy-done, bf16[2,288,3584]{2,1,0:T(8,128)(2,1)S(1)} %fusion), kind=kLoop, calls=%fused_computation.2 | loop fusion | flops 7225344 | bytes 8257536 | tf_op jit(solution)/shard_map/convert_element_type | solution.py:53
  184.3 2.0 %collective-permute-done.7 = bf16[2,128,288]{1,2,0:T(8,128)(2,1)S(1)} collective-permute-done((bf16[2,128,288]{1,2,0:T(8,128)(2,1)S(1)}, bf16[2,128,288]{1,2,0:T(8,128)(2,1)S(1)}, u32[]{:S(2)}, u32[]{:S(2)}) %collective-permute-start.7) | collective-permute-done | bytes 147488 | tf_op jit(solution)/shard_map/ppermute | solution.py:16
  186.3 0.7 maximum_bitcast_fusion
  (2 shorter events, 0.1 us)
Async XLA Ops:
  7.2 138.2 %all-gather.2.cloned.1.call-start = ((), (), s32[]{:S(2)}) async-start(), calls=%async_computation | async-start | bytes 3784704 | tf_op jit(solution)/shard_map/all_gather | solution.py:43
  10.7 8.9 %collective-permute-start = (bf16[2,51200]{1,0:T(2,128)(2,1)S(1)}, bf16[2,51200]{1,0:T(2,128)(2,1)S(1)}, u32[]{:S(2)}, u32[]{:S(2)}) collective-permute-start(bf16[2,51200]{1,0:T(2,128)(2,1)S(1)} %pad_maximum_fusion), channel_id=1, source_target_pairs={{0,32},{32,0},{64,96},{96,64},{128,160},{160,128},{192,224},{224,1... | collective-permute-start | bytes 614408 | tf_op jit(solution)/shard_map/ppermute | solution.py:16
  19.6 14.0 %collective-permute-start.1 = (bf16[2,51200]{1,0:T(2,128)(2,1)S(1)}, bf16[2,51200]{1,0:T(2,128)(2,1)S(1)}, u32[]{:S(2)}, u32[]{:S(2)}) collective-permute-start(bf16[2,51200]{1,0:T(2,128)(2,1)S(1)} %collective-permute-done), channel_id=1, source_target_pairs={{0,64},{64,0},{32,96},{96,32},{128,192},{192,128},{160,224},{224,1... | collective-permute-start | bytes 614408 | tf_op jit(solution)/shard_map/ppermute | solution.py:16
  33.6 7.8 %collective-permute-start.2 = (bf16[2,51200]{1,0:T(2,128)(2,1)S(1)}, bf16[2,51200]{1,0:T(2,128)(2,1)S(1)}, u32[]{:S(2)}, u32[]{:S(2)}) collective-permute-start(bf16[2,51200]{1,0:T(2,128)(2,1)S(1)} %collective-permute-done.1), channel_id=1, source_target_pairs={{0,128},{128,0},{32,160},{160,32},{64,192},{192,64},{96,224},{224,... | collective-permute-start | bytes 614408 | tf_op jit(solution)/shard_map/ppermute | solution.py:16
  41.4 9.1 %collective-permute-start.3 = (bf16[2,51200]{1,0:T(2,128)(2,1)S(1)}, bf16[2,51200]{1,0:T(2,128)(2,1)S(1)}, u32[]{:S(2)}, u32[]{:S(2)}) collective-permute-start(bf16[2,51200]{1,0:T(2,128)(2,1)S(1)} %collective-permute-done.2), channel_id=1, source_target_pairs={{0,256},{256,0},{32,288},{288,32},{64,320},{320,64},{96,352},{352,... | collective-permute-start | bytes 614408 | tf_op jit(solution)/shard_map/ppermute | solution.py:16
  149.4 7.9 %collective-permute-start.4 = (bf16[2,128,288]{1,2,0:T(8,128)(2,1)S(1)}, bf16[2,128,288]{1,2,0:T(8,128)(2,1)S(1)}, u32[]{:S(2)}, u32[]{:S(2)}) collective-permute-start(bf16[2,128,288]{1,2,0:T(8,128)(2,1)S(1)} %get-tuple-element.5), channel_id=1, source_target_pairs={{0,32},{32,0},{64,96},{96,64},{128,160},{160,128},{192,224},{224,1... | collective-permute-start | bytes 442376 | tf_op jit(solution)/shard_map/ppermute | solution.py:16
  157.3 11.2 %collective-permute-start.5 = (bf16[2,128,288]{1,2,0:T(8,128)(2,1)S(1)}, bf16[2,128,288]{1,2,0:T(8,128)(2,1)S(1)}, u32[]{:S(2)}, u32[]{:S(2)}) collective-permute-start(bf16[2,128,288]{1,2,0:T(8,128)(2,1)S(1)} %collective-permute-done.4), channel_id=1, source_target_pairs={{0,64},{64,0},{32,96},{96,32},{128,192},{192,128},{160,224},{224,1... | collective-permute-start | bytes 442376 | tf_op jit(solution)/shard_map/ppermute | solution.py:16
  168.5 9.0 %collective-permute-start.6 = (bf16[2,128,288]{1,2,0:T(8,128)(2,1)S(1)}, bf16[2,128,288]{1,2,0:T(8,128)(2,1)S(1)}, u32[]{:S(2)}, u32[]{:S(2)}) collective-permute-start(bf16[2,128,288]{1,2,0:T(8,128)(2,1)S(1)} %collective-permute-done.5), channel_id=1, source_target_pairs={{0,128},{128,0},{32,160},{160,32},{64,192},{192,64},{96,224},{224,... | collective-permute-start | bytes 442376 | tf_op jit(solution)/shard_map/ppermute | solution.py:16
  173.4 8.8 %copy-start = (bf16[1,288,3584]{2,1,0:T(8,128)(2,1)S(1)}, bf16[1,288,3584]{2,1,0:T(8,128)(2,1)}, u32[]{:S(2)}) copy-start(bf16[1,288,3584]{2,1,0:T(8,128)(2,1)} %param.6) | copy-start | bytes 6193156
  177.5 8.8 %collective-permute-start.7 = (bf16[2,128,288]{1,2,0:T(8,128)(2,1)S(1)}, bf16[2,128,288]{1,2,0:T(8,128)(2,1)S(1)}, u32[]{:S(2)}, u32[]{:S(2)}) collective-permute-start(bf16[2,128,288]{1,2,0:T(8,128)(2,1)S(1)} %collective-permute-done.6), channel_id=1, source_target_pairs={{0,256},{256,0},{32,288},{288,32},{64,320},{320,64},{96,352},{352,... | collective-permute-start | bytes 442376 | tf_op jit(solution)/shard_map/ppermute | solution.py:16
Sparse Core Ops, SparseCore 0:
  51.6 93.7 all-gather.1
where the time goes:
time: 194 us
  waiting for transfers between devices  131 us (68%)
  starting transfers between devices  32.5 us (17%)
  between operations  14.2 us (7%)
  matrix products  8.07 us (4%)
  other arithmetic  5.64 us (3%)
  local copies, waits for them, and re-layouts  2.22 us (1%)
    all_gather x1, waiting for transfers between devices, shards(): piece = lax.all_gather(both_masked, 'dp', axis=2, tiled=True)  93.9 us
    ppermute x8, waiting for transfers between devices, from_partner(): return lax.ppermute(block, axis, route)  37.4 us
    ppermute x8, starting transfers between devices, from_partner(): return lax.ppermute(block, axis, route)  32.5 us
    dot_general x1, matrix products, shards(): jnp.einsum('rmkh,rmkd->rhd', both_hidden, piece, preferred_element_type=j...  4.1 us
    dot_general x1, matrix products, shards(): jnp.einsum('rmkd,hd->rmkh', piece, own_weight, preferred_element_type=jnp...  3.97 us
  transfers between devices with their start and end apart: 9, of which 8 were waited for; matrix products, arithmetic and copies ran while one was open for 4% of the time, Pallas kernels for 0%

commit v1 on v0

--- a/solution.py
+++ b/solution.py
@@ -40,7 +40,9 @@
     mirror_masked, mirror_hidden = (mirror_masked, mirror_hidden)
     both_masked = jnp.stack([masked[0, 0], mirror_masked], axis=0)
     both_hidden = jnp.stack([hidden[0, 0], mirror_hidden], axis=0)
-    piece = lax.all_gather(both_masked, "dp", axis=2, tiled=True)
+    piece = jnp.concatenate(
+        lax.all_to_all(jnp.stack([both_masked] * lax.axis_size("dp")), "dp", 0, 0), axis=2
+    )
     rows_out = jnp.einsum("rmkd,hd->rmkh", piece, own_weight, preferred_element_type=jnp.float32)
     grad_acc = rows_out
     weight_acc = jnp.einsum(

time: 194 us -> 278 us (1.43)
  the two profiles are of different devices: /device:TPU:4 before, /device:TPU:16 now
where the time goes in v1:
time: 278 us; the launch traced here: 277 us
  blocking collectives  181 us (65%)
  waiting for transfers between devices  42.6 us (15%)
  starting transfers between devices  26.9 us (10%)
  local copies, waits for them, and re-layouts  13.9 us (5%)
  matrix products  6.57 us (2%)
  other arithmetic  4.94 us (2%)
    all_to_all x1, blocking collectives, shards(): lax.all_to_all(jnp.stack([both_masked] * lax.axis_size('dp')), 'dp', 0, 0)  181 us
    ppermute x8, waiting for transfers between devices, from_partner(): return lax.ppermute(block, axis, route)  42.6 us
    ppermute x8, starting transfers between devices, from_partner(): return lax.ppermute(block, axis, route)  26.9 us
    reshape x2, local copies, waits for them, and re-layouts, shards(): jnp.concatenate(lax.all_to_all(jnp.stack([both_masked] * lax.axis_size('d...  9.95 us
  transfers between devices with their start and end apart: 8, of which 8 were waited for; matrix products, arithmetic and copies ran while one was open for 2% of the time, Pallas kernels for 0%

profile of v1, /device:TPU:16, one launch (start us, length us, event | category | flops | bytes accessed | tf_op | source)
XLA Modules:
  0.0 277.0 jit_solution(10693454347659125273)
XLA Ops:
  0.6 0.8 iota_compare_fusion
  1.4 1.0 broadcast_select_fusion
  2.5 1.0 slice_bitcast_fusion.1
  3.5 0.2 copy.8
  3.7 0.3 reshape_squeeze.7
  4.0 0.2 pad_maximum_fusion
  4.2 3.8 %collective-permute-start = (bf16[2,51200]{1,0:T(2,128)(2,1)S(1)}, bf16[2,51200]{1,0:T(2,128)(2,1)S(1)}, u32[]{:S(2)}, u32[]{:S(2)}) collective-permute-start(bf16[2,51200]{1,0:T(2,128)(2,1)S(1)} %pad_maximum_fusion), channel_id=1, source_target_pairs={{0,32},{32,0},{64,96},{96,64},{128,160},{160,128},{192,224},{224,1... | collective-permute-start | bytes 614408 | tf_op jit(solution)/shard_map/ppermute | solution.py:16
  8.0 5.1 %collective-permute-done = bf16[2,51200]{1,0:T(2,128)(2,1)S(1)} collective-permute-done((bf16[2,51200]{1,0:T(2,128)(2,1)S(1)}, bf16[2,51200]{1,0:T(2,128)(2,1)S(1)}, u32[]{:S(2)}, u32[]{:S(2)}) %collective-permute-start) | collective-permute-done | bytes 204832 | tf_op jit(solution)/shard_map/ppermute | solution.py:16
  13.1 5.2 %collective-permute-start.1 = (bf16[2,51200]{1,0:T(2,128)(2,1)S(1)}, bf16[2,51200]{1,0:T(2,128)(2,1)S(1)}, u32[]{:S(2)}, u32[]{:S(2)}) collective-permute-start(bf16[2,51200]{1,0:T(2,128)(2,1)S(1)} %collective-permute-done), channel_id=1, source_target_pairs={{0,64},{64,0},{32,96},{96,32},{128,192},{192,128},{160,224},{224,1... | collective-permute-start | bytes 614408 | tf_op jit(solution)/shard_map/ppermute | solution.py:16
  18.3 8.8 %collective-permute-done.1 = bf16[2,51200]{1,0:T(2,128)(2,1)S(1)} collective-permute-done((bf16[2,51200]{1,0:T(2,128)(2,1)S(1)}, bf16[2,51200]{1,0:T(2,128)(2,1)S(1)}, u32[]{:S(2)}, u32[]{:S(2)}) %collective-permute-start.1) | collective-permute-done | bytes 204832 | tf_op jit(solution)/shard_map/ppermute | solution.py:16
  27.0 3.2 %collective-permute-start.2 = (bf16[2,51200]{1,0:T(2,128)(2,1)S(1)}, bf16[2,51200]{1,0:T(2,128)(2,1)S(1)}, u32[]{:S(2)}, u32[]{:S(2)}) collective-permute-start(bf16[2,51200]{1,0:T(2,128)(2,1)S(1)} %collective-permute-done.1), channel_id=1, source_target_pairs={{0,128},{128,0},{32,160},{160,32},{64,192},{192,64},{96,224},{224,... | collective-permute-start | bytes 614408 | tf_op jit(solution)/shard_map/ppermute | solution.py:16
  30.2 4.7 %collective-permute-done.2 = bf16[2,51200]{1,0:T(2,128)(2,1)S(1)} collective-permute-done((bf16[2,51200]{1,0:T(2,128)(2,1)S(1)}, bf16[2,51200]{1,0:T(2,128)(2,1)S(1)}, u32[]{:S(2)}, u32[]{:S(2)}) %collective-permute-start.2) | collective-permute-done | bytes 204832 | tf_op jit(solution)/shard_map/ppermute | solution.py:16
  34.9 2.4 collective-permute-start.3
  37.3 6.8 %collective-permute-done.3 = bf16[2,51200]{1,0:T(2,128)(2,1)S(1)} collective-permute-done((bf16[2,51200]{1,0:T(2,128)(2,1)S(1)}, bf16[2,51200]{1,0:T(2,128)(2,1)S(1)}, u32[]{:S(2)}, u32[]{:S(2)}) %collective-permute-start.3) | collective-permute-done | bytes 204832 | tf_op jit(solution)/shard_map/ppermute | solution.py:16
  44.1 0.1 pad_maximum_fusion.1
  44.2 1.6 stack.11
  45.9 181.3 %all_to_all.5 = bf16[32,2,2,4,3584]{4,3,2,1,0:T(4,128)(2,1)S(1)} all-to-all(bf16[32,2,2,4,3584]{4,3,2,1,0:T(4,128)(2,1)S(1)} %stack.11), channel_id=1, replica_groups=mesh['pipe'=16,'dp'=32] {'dp'}, dimensions={0} | all-to-all | bytes 7340032 | tf_op jit(solution)/shard_map/all_to_all | solution.py:44
  227.2 3.1 %copy.9 = bf16[2,2,32,4,3584]{4,3,2,1,0:T(4,128)(2,1)} copy(bf16[2,2,32,4,3584]{4,3,1,0,2:T(4,128)(2,1)S(1)} %bitcast.35) | data formatting | bytes 7340032 | tf_op jit(solution)/shard_map/reshape | solution.py:43
  230.3 0.0 copy-start
  230.3 6.9 %reshape.22 = bf16[2,2,128,3584]{3,2,1,0:T(8,128)(2,1)} reshape(bf16[2,2,32,4,3584]{4,3,2,1,0:T(4,128)(2,1)} %copy.9) | data formatting | bytes 7340032 | tf_op jit(solution)/shard_map/reshape | solution.py:43
  237.2 0.0 copy-done
  237.2 3.3 %fusion.6 = bf16[2,2,128,288]{2,3,1,0:T(8,128)(2,1)S(1)} fusion(bf16[2,2,128,3584]{3,2,1,0:T(8,128)(2,1)} %reshape.22, bf16[1,288,3584]{2,1,0:T(8,128)(2,1)S(1)} %copy-done), kind=kOutput, calls=%fused_computation.6 | convolution fusion | flops 1057259520 | bytes 6029312 | tf_op jit(solution)/shard_map/rmkd,hd->rmkh/dot_general | solution.py:46
  240.5 1.9 collective-permute-start.4
  242.4 6.4 %collective-permute-done.4 = bf16[2,128,288]{1,2,0:T(8,128)(2,1)S(1)} collective-permute-done((bf16[2,128,288]{1,2,0:T(8,128)(2,1)S(1)}, bf16[2,128,288]{1,2,0:T(8,128)(2,1)S(1)}, u32[]{:S(2)}, u32[]{:S(2)}) %collective-permute-start.4) | collective-permute-done | bytes 147488 | tf_op jit(solution)/shard_map/ppermute | solution.py:16
  248.8 5.0 %collective-permute-start.5 = (bf16[2,128,288]{1,2,0:T(8,128)(2,1)S(1)}, bf16[2,128,288]{1,2,0:T(8,128)(2,1)S(1)}, u32[]{:S(2)}, u32[]{:S(2)}) collective-permute-start(bf16[2,128,288]{1,2,0:T(8,128)(2,1)S(1)} %collective-permute-done.4), channel_id=1, source_target_pairs={{0,64},{64,0},{32,96},{96,32},{128,192},{192,128},{160,224},{224,1... | collective-permute-start | bytes 442376 | tf_op jit(solution)/shard_map/ppermute | solution.py:16
  253.8 0.1 slice.45
  253.9 0.3 stack_reshape.7
  254.2 0.2 copy.10
  254.4 5.7 %collective-permute-done.5 = bf16[2,128,288]{1,2,0:T(8,128)(2,1)S(1)} collective-permute-done((bf16[2,128,288]{1,2,0:T(8,128)(2,1)S(1)}, bf16[2,128,288]{1,2,0:T(8,128)(2,1)S(1)}, u32[]{:S(2)}, u32[]{:S(2)}) %collective-permute-start.5) | collective-permute-done | bytes 147488 | tf_op jit(solution)/shard_map/ppermute | solution.py:16
  260.1 3.2 %collective-permute-start.6 = (bf16[2,128,288]{1,2,0:T(8,128)(2,1)S(1)}, bf16[2,128,288]{1,2,0:T(8,128)(2,1)S(1)}, u32[]{:S(2)}, u32[]{:S(2)}) collective-permute-start(bf16[2,128,288]{1,2,0:T(8,128)(2,1)S(1)} %collective-permute-done.5), channel_id=1, source_target_pairs={{0,128},{128,0},{32,160},{160,32},{64,192},{192,64},{96,224},{224,... | collective-permute-start | bytes 442376 | tf_op jit(solution)/shard_map/ppermute | solution.py:16
  263.3 3.3 %fusion = bf16[2,288,3584]{2,1,0:T(8,128)(2,1)S(1)} fusion(bf16[2,2,128,3584]{3,2,1,0:T(8,128)(2,1)} %reshape.22, bf16[1,2,128,288]{2,3,1,0:T(8,128)(2,1)S(1)} %copy.10, bf16[1,2,128,288]{2,3,1,0:T(8,128)(2,1)S(1)} %get-tuple-element.2), kind=kOutput, calls=%fused_computation.1 | convolution fusion | flops 1061240832 | bytes 8093696 | tf_op jit(solution)/shard_map/rmkh,rmkd->rhd/dot_general | solution.py:48
  266.6 1.2 collective-permute-done.6
  267.7 2.2 collective-permute-start.7
  270.0 2.2 subtract_convert_fusion
  272.2 4.1 %collective-permute-done.7 = bf16[2,128,288]{1,2,0:T(8,128)(2,1)S(1)} collective-permute-done((bf16[2,128,288]{1,2,0:T(8,128)(2,1)S(1)}, bf16[2,128,288]{1,2,0:T(8,128)(2,1)S(1)}, u32[]{:S(2)}, u32[]{:S(2)}) %collective-permute-start.7) | collective-permute-done | bytes 147488 | tf_op jit(solution)/shard_map/ppermute | solution.py:16
  276.3 0.7 maximum_bitcast_fusion
  (5 shorter events, 0.2 us)
Async XLA Ops:
  4.2 8.9 %collective-permute-start = (bf16[2,51200]{1,0:T(2,128)(2,1)S(1)}, bf16[2,51200]{1,0:T(2,128)(2,1)S(1)}, u32[]{:S(2)}, u32[]{:S(2)}) collective-permute-start(bf16[2,51200]{1,0:T(2,128)(2,1)S(1)} %pad_maximum_fusion), channel_id=1, source_target_pairs={{0,32},{32,0},{64,96},{96,64},{128,160},{160,128},{192,224},{224,1... | collective-permute-start | bytes 614408 | tf_op jit(solution)/shard_map/ppermute | solution.py:16
  13.1 14.0 %collective-permute-start.1 = (bf16[2,51200]{1,0:T(2,128)(2,1)S(1)}, bf16[2,51200]{1,0:T(2,128)(2,1)S(1)}, u32[]{:S(2)}, u32[]{:S(2)}) collective-permute-start(bf16[2,51200]{1,0:T(2,128)(2,1)S(1)} %collective-permute-done), channel_id=1, source_target_pairs={{0,64},{64,0},{32,96},{96,32},{128,192},{192,128},{160,224},{224,1... | collective-permute-start | bytes 614408 | tf_op jit(solution)/shard_map/ppermute | solution.py:16
  27.0 7.8 %collective-permute-start.2 = (bf16[2,51200]{1,0:T(2,128)(2,1)S(1)}, bf16[2,51200]{1,0:T(2,128)(2,1)S(1)}, u32[]{:S(2)}, u32[]{:S(2)}) collective-permute-start(bf16[2,51200]{1,0:T(2,128)(2,1)S(1)} %collective-permute-done.1), channel_id=1, source_target_pairs={{0,128},{128,0},{32,160},{160,32},{64,192},{192,64},{96,224},{224,... | collective-permute-start | bytes 614408 | tf_op jit(solution)/shard_map/ppermute | solution.py:16
  34.9 9.1 %collective-permute-start.3 = (bf16[2,51200]{1,0:T(2,128)(2,1)S(1)}, bf16[2,51200]{1,0:T(2,128)(2,1)S(1)}, u32[]{:S(2)}, u32[]{:S(2)}) collective-permute-start(bf16[2,51200]{1,0:T(2,128)(2,1)S(1)} %collective-permute-done.2), channel_id=1, source_target_pairs={{0,256},{256,0},{32,288},{288,32},{64,320},{320,64},{96,352},{352,... | collective-permute-start | bytes 614408 | tf_op jit(solution)/shard_map/ppermute | solution.py:16
  230.3 6.9 %copy-start = (bf16[1,288,3584]{2,1,0:T(8,128)(2,1)S(1)}, bf16[1,288,3584]{2,1,0:T(8,128)(2,1)}, u32[]{:S(2)}) copy-start(bf16[1,288,3584]{2,1,0:T(8,128)(2,1)} %param.6) | copy-start | bytes 6193156
  240.5 8.3 %collective-permute-start.4 = (bf16[2,128,288]{1,2,0:T(8,128)(2,1)S(1)}, bf16[2,128,288]{1,2,0:T(8,128)(2,1)S(1)}, u32[]{:S(2)}, u32[]{:S(2)}) collective-permute-start(bf16[2,128,288]{1,2,0:T(8,128)(2,1)S(1)} %get-tuple-element.5), channel_id=1, source_target_pairs={{0,32},{32,0},{64,96},{96,64},{128,160},{160,128},{192,224},{224,1... | collective-permute-start | bytes 442376 | tf_op jit(solution)/shard_map/ppermute | solution.py:16
  248.8 11.3 %collective-permute-start.5 = (bf16[2,128,288]{1,2,0:T(8,128)(2,1)S(1)}, bf16[2,128,288]{1,2,0:T(8,128)(2,1)S(1)}, u32[]{:S(2)}, u32[]{:S(2)}) collective-permute-start(bf16[2,128,288]{1,2,0:T(8,128)(2,1)S(1)} %collective-permute-done.4), channel_id=1, source_target_pairs={{0,64},{64,0},{32,96},{96,32},{128,192},{192,128},{160,224},{224,1... | collective-permute-start | bytes 442376 | tf_op jit(solution)/shard_map/ppermute | solution.py:16
  260.1 7.7 %collective-permute-start.6 = (bf16[2,128,288]{1,2,0:T(8,128)(2,1)S(1)}, bf16[2,128,288]{1,2,0:T(8,128)(2,1)S(1)}, u32[]{:S(2)}, u32[]{:S(2)}) collective-permute-start(bf16[2,128,288]{1,2,0:T(8,128)(2,1)S(1)} %collective-permute-done.5), channel_id=1, source_target_pairs={{0,128},{128,0},{32,160},{160,32},{64,192},{192,64},{96,224},{224,... | collective-permute-start | bytes 442376 | tf_op jit(solution)/shard_map/ppermute | solution.py:16
  267.7 8.5 %collective-permute-start.7 = (bf16[2,128,288]{1,2,0:T(8,128)(2,1)S(1)}, bf16[2,128,288]{1,2,0:T(8,128)(2,1)S(1)}, u32[]{:S(2)}, u32[]{:S(2)}) collective-permute-start(bf16[2,128,288]{1,2,0:T(8,128)(2,1)S(1)} %collective-permute-done.6), channel_id=1, source_target_pairs={{0,256},{256,0},{32,288},{288,32},{64,320},{320,64},{96,352},{352,... | collective-permute-start | bytes 442376 | tf_op jit(solution)/shard_map/ppermute | solution.py:16
